TPU v7x, 32 devices: a whole 2x2x4 slice. The times are simulated.
32 devices in a mesh: member: 2 (over y), lon: 8 (over z, x), lat: 2 (over core).
Axes of the slice: x: 2, y: 2, z: 4, core: 2. Of those that a mesh axis runs over, the one named last changes fastest.
Arguments:
- fields: bfloat16 [1280, 32, 128], P('member', 'lat', 'lon'), parts along dimension 0, may hold values from -6 to 6
- support_rows: int32 [7, 32, 16], replicated, may hold values from -1 to 1
- support_lons: int32 [7, 32, 16], replicated, may hold values from -64 to 64, as said below
- support_weights: float32 [7, 32, 16], replicated, may hold values from -1.5 to 1.5
- mix_weight: bfloat16 [7, 640, 640], replicated, may hold values from -0.09375 to 0.09375
- norm_gain: float32 [640], replicated, may hold values from 0.1 to 1.9
- up_weight: bfloat16 [640, 1280], replicated, may hold values from -0.25 to 0.25
- down_weight: bfloat16 [1280, 640], replicated, may hold values from -0.15625 to 0.15625
Outputs:
- output: bfloat16 [1280, 32, 128], P('member', 'lat', 'lon'), parts along dimension 0
There are 2 independent parts, one for each index of `member`. A program takes and returns all parts, laid end to end along the dimension named above; an argument that names none is the same for every part. Nothing has to cross between parts.
Inputs may be any that keep to these rules, and one draw needn't show every extreme that they name: `support_lons`: at output row i every offset lies within plus or minus min(64, 4 * 32 // min(i + 1, 32 - i)); in every basis filter the first pole row has an entry at -(64) and the last pole row one at 64.
All inputs are finite; a program needn't handle non-finite values.
Results may differ from a plain program's by a relative error of at most 0.0095.
Values may be sent and summed in bfloat16 or wider, within the bound.
A program may use at most 128 MiB of HBM per device.

v0:
```python
import math

import jax
import jax.numpy as jnp
from jax import lax
from jax.sharding import PartitionSpec as P

full_turn = 2.0 * math.pi
norm_eps = 1e-05


def extended(block, sides, width):
    for axis, dim in sides:
        count = lax.axis_size(axis)
        forward = [(i, i + 1) for i in range(count - 1)]
        backward = [(target, source) for source, target in forward]
        low = lax.ppermute(
            lax.slice_in_dim(block, block.shape[dim] - width, None, axis=dim), axis, forward
        )
        high = lax.ppermute(lax.slice_in_dim(block, 0, width, axis=dim), axis, backward)
        block = jnp.concatenate([low, block, high], axis=dim)
    return block


def transform_tables(lon_total):
    lon_half = lon_total // 2
    column = lax.broadcasted_iota(jnp.int32, (lon_total, lon_total), 1)
    sample = lax.broadcasted_iota(jnp.int32, (lon_total, lon_total), 0)
    cos_freq = jnp.where(column == 1, lon_half, column // 2)
    sin_freq = column // 2
    cos_angle = jnp.mod(sample * cos_freq, lon_total).astype(jnp.float32) * (full_turn / lon_total)
    sin_angle = jnp.mod(sample * sin_freq, lon_total).astype(jnp.float32) * (full_turn / lon_total)
    odd_column = (jnp.mod(column, 2) == 1) & (column != 1)
    forward = jnp.where(odd_column, jnp.sin(sin_angle), jnp.cos(cos_angle))
    column_ids = jnp.arange(lon_total, dtype=jnp.int32)
    weight_col = jnp.where(column_ids <= 1, 1.0, 2.0).astype(jnp.float32) / lon_total
    inverse = forward.T * weight_col[:, None]
    return (forward, inverse)


def partner(spectrum):
    pairs = spectrum.reshape(spectrum.shape[:-1] + (spectrum.shape[-1] // 2, 2))
    swapped = jnp.stack([pairs[..., 1], -pairs[..., 0]], axis=-1)
    return swapped.reshape(spectrum.shape)


def filter_spectra(row_offsets, lon_offsets, weights, columns, lon_total):
    lon_half = lon_total // 2
    cos_freq = jnp.where(columns == 1, lon_half, columns // 2)
    sin_freq = columns // 2
    cos_angle = jnp.mod(lon_offsets[..., None] * cos_freq, lon_total).astype(jnp.float32) * (
        full_turn / lon_total
    )
    sin_angle = jnp.mod(lon_offsets[..., None] * sin_freq, lon_total).astype(jnp.float32) * (
        full_turn / lon_total
    )
    offsets = jnp.array([-1, 0, 1], jnp.int32)
    picked = jnp.where(row_offsets[..., None] == offsets, weights[..., None], 0.0)
    direct = jnp.einsum(
        "kisr,kisn->kirn", picked, jnp.cos(cos_angle), precision=lax.Precision.HIGHEST
    )
    cross_part = jnp.einsum(
        "kisr,kisn->kirn", picked, jnp.sin(sin_angle), precision=lax.Precision.HIGHEST
    )
    return (direct, cross_part)


def spectral_product(spectrum, direct, cross_part, rows_out):
    mirrored = partner(spectrum)
    summed = None
    for position in range(3):
        shifted_spec = spectrum[:, position : position + rows_out]
        shifted_pair = mirrored[:, position : position + rows_out]
        piece = (
            shifted_spec[None] * direct[:, None, :, position]
            + shifted_pair[None] * cross_part[:, None, :, position]
        )
        summed = piece if summed is None else summed + piece
    return summed


def filtered(spectrum, columns, support_rows, support_lons, support_weights, row_start, lon_total):
    lat_rows = spectrum.shape[1]
    padded_rows = jnp.pad(support_rows, ((0, 0), (1, 1), (0, 0)))
    padded_lons = jnp.pad(support_lons, ((0, 0), (1, 1), (0, 0)))
    padded_weights = jnp.pad(support_weights, ((0, 0), (1, 1), (0, 0)))
    widened = jnp.pad(spectrum.astype(jnp.float32), ((0, 0), (2, 2), (0, 0)))
    row_sel = lax.dynamic_slice_in_dim(padded_rows, row_start, lat_rows + 2, 1)
    lon_sel = lax.dynamic_slice_in_dim(padded_lons, row_start, lat_rows + 2, 1)
    weight_sel = lax.dynamic_slice_in_dim(padded_weights, row_start, lat_rows + 2, 1)
    direct, cross_part = filter_spectra(row_sel, lon_sel, weight_sel, columns, lon_total)
    product_all = spectral_product(widened, direct, cross_part, lat_rows + 2)
    edge_terms = jnp.concatenate([product_all[:, :, :1], product_all[:, :, lat_rows + 1 :]], axis=2)
    framed = extended(edge_terms.astype(jnp.bfloat16), (("lat", 2),), 1).astype(edge_terms.dtype)
    from_above = jnp.pad(framed[:, :, 0:1], ((0, 0), (0, 0), (0, lat_rows - 1), (0, 0)))
    from_below = jnp.pad(framed[:, :, 3:4], ((0, 0), (0, 0), (lat_rows - 1, 0), (0, 0)))
    product = product_all[:, :, 1 : lat_rows + 1] + from_above + from_below
    return product.astype(jnp.bfloat16)


def on_device(
    fields,
    support_rows,
    support_lons,
    support_weights,
    mix_weight,
    norm_gain,
    up_weight,
    down_weight,
):
    channels, lat_rows, lon_cols = fields.shape
    moved = lax.all_to_all(fields, "lon", split_axis=0, concat_axis=2, tiled=True)
    local_channels = moved.shape[0]
    lon_total = moved.shape[2]
    forward, inverse = transform_tables(lon_total)
    row_start = lax.axis_index("lat") * lat_rows
    spectrum = jnp.dot(
        moved.reshape(-1, lon_total),
        forward,
        precision=lax.Precision.HIGH,
        preferred_element_type=jnp.float32,
    )
    spectrum = spectrum.reshape(local_channels, lat_rows, lon_total).astype(jnp.bfloat16)
    bands = lax.all_to_all(spectrum, "lon", split_axis=2, concat_axis=0, tiled=True)
    columns = lax.axis_index("lon") * lon_cols + jnp.arange(lon_cols, dtype=jnp.int32)
    product = filtered(
        bands, columns, support_rows, support_lons, support_weights, row_start, lon_total
    )
    mixed_spec = lax.dot_general(
        mix_weight.reshape(-1, channels),
        product.reshape(-1, lat_rows * lon_cols),
        (((0,), (0,)), ((), ())),
        preferred_element_type=jnp.float32,
    )
    mixed_spec = mixed_spec.reshape(channels, lat_rows, lon_cols)
    gathered_spec = lax.all_to_all(
        mixed_spec.astype(jnp.bfloat16), "lon", split_axis=0, concat_axis=2, tiled=True
    ).astype(mixed_spec.dtype)
    spatial = jnp.dot(
        gathered_spec.reshape(-1, lon_total),
        inverse,
        precision=lax.Precision.HIGHEST,
        preferred_element_type=jnp.float32,
    )
    spatial = spatial.reshape(local_channels, lat_rows, lon_total)
    mixed = (
        lax.all_to_all(spatial.astype(jnp.bfloat16), "lon", split_axis=2, concat_axis=0, tiled=True)
        .astype(spatial.dtype)
        .reshape(channels, lat_rows * lon_cols)
    )
    latent = fields.reshape(channels, lat_rows * lon_cols).astype(jnp.float32) + mixed
    row_mean = jnp.mean(latent, axis=0)
    variance = jnp.mean(jnp.square(latent - row_mean), axis=0)
    normed = ((latent - row_mean) * lax.rsqrt(variance + norm_eps) * norm_gain[:, None]).astype(
        jnp.bfloat16
    )
    hidden = jax.nn.gelu(
        lax.dot_general(
            up_weight, normed, (((0,), (0,)), ((), ())), preferred_element_type=jnp.float32
        ),
        approximate=False,
    ).astype(jnp.bfloat16)
    output = latent + lax.dot_general(
        down_weight, hidden, (((0,), (0,)), ((), ())), preferred_element_type=jnp.float32
    )
    return output.astype(jnp.bfloat16).reshape(channels, lat_rows, lon_cols)


def solution(mesh):
    in_specs = (P("member", "lat", "lon"), P(), P(), P(), P(), P(), P(), P())
    out_specs = P("member", "lat", "lon")
    return jax.shard_map(
        on_device, mesh=mesh, in_specs=in_specs, out_specs=out_specs, check_vma=False
    )
```

profile of v0, /device:TPU:0, one launch (start us, length us, event | category | flops | bytes accessed | tf_op | source)
XLA Modules:
  0.0 136.9 jit_solution(329501171711781699)
XLA Ops:
  0.0 3.7 %copy.90 = bf16[640,16,16]{2,1,0:T(8,128)(2,1)} copy(bf16[640,16,16]{0,2,1:T(8,128)(2,1)} %param.9) | data formatting | bytes 655360 | tf_op args[0]
  3.7 5.1 %reshape.133 = bf16[8,2,10240]{2,1,0:T(2,128)(2,1)} reshape(bf16[640,16,16]{2,1,0:T(8,128)(2,1)} %copy.90) | data formatting | bytes 655360
  8.8 7.4 %all-to-all-start = ((bf16[8,2,10240]{2,1,0:T(2,128)(2,1)}), bf16[8,2,10240]{2,1,0:T(2,128)(2,1)S(1)}, u32[]{:S(2)}, u32[]{:S(2)}) async-start(bf16[8,2,10240]{2,1,0:T(2,128)(2,1)} %reshape.133), calls=%async_computation | async-start | bytes 655360 | tf_op jit(solution)/shard_map/all_to_all | solution.py:112
  16.2 0.1 pad_dynamic-slice_fusion
  16.3 0.1 copy.96
  16.4 0.1 copy.98
  16.7 0.1 copy.97
  16.8 5.3 %fusion.26 = f32[7,18,3,16]{3,2,1,0:T(4,128)S(1)} fusion(s32[16]{0:T(128)S(1)} %get-tuple-element.26, s32[7,18,16]{2,1,0:T(8,128)S(1)} %copy.98, f32[7,18,16]{2,1,0:T(8,128)S(1)} %copy.97, s32[7,18,16]{2,1,0:T(8,128)S(1)} %copy.96, s32[3]{0:T(128)S(1)} %copy-done.15), kind=kOutput, calls=%fused_computation.50 | convolution fusion | flops 1624896 | bytes 48460 | tf_op jit(solution)/shard_map/kisr,kisn->kirn/dot_general | solution.py:59
  22.2 4.3 %all-to-all-done = bf16[8,2,10240]{2,1,0:T(2,128)(2,1)S(1)} async-done(((bf16[8,2,10240]{2,1,0:T(2,128)(2,1)}), bf16[8,2,10240]{2,1,0:T(2,128)(2,1)S(1)}, u32[]{:S(2)}, u32[]{:S(2)}) %all-to-all-start) | async-done | bytes 327712 | tf_op jit(solution)/shard_map/all_to_all | solution.py:112
  26.5 2.9 %reshape.134 = bf16[640,16,16]{2,1,0:T(8,128)(2,1)} reshape(bf16[8,2,10240]{2,1,0:T(2,128)(2,1)S(1)} %all-to-all-done) | data formatting | bytes 655360
  29.4 6.3 %copy.130 = bf16[8,80,16,16]{3,0,2,1:T(8,128)(2,1)} copy(bf16[8,80,16,16]{3,2,1,0:T(8,128)(2,1)} %bitcast.142) | data formatting | bytes 655360 | tf_op jit(solution)/shard_map/all_to_all | solution.py:112
  35.7 3.5 %reshape.121 = bf16[1280,128]{1,0:T(8,128)(2,1)S(1)} reshape(bf16[80,16,8,16]{3,2,1,0:T(8,128)(2,1)} %bitcast.143) | data formatting | bytes 655360 | tf_op jit(solution)/shard_map/reshape | solution.py:118
  39.2 0.9 fusion.2
  40.1 0.2 copy.92
  40.3 1.3 copy.93
  41.7 3.7 %all-to-all-start.1 = ((bf16[80,16,128]{0,1,2:T(8,128)(2,1)}), bf16[80,16,128]{0,1,2:T(8,128)(2,1)S(1)}, u32[]{:S(2)}, u32[]{:S(2)}) async-start(bf16[80,16,128]{0,1,2:T(8,128)(2,1)} %copy.93), calls=%async_computation.1 | async-start | bytes 1048576 | tf_op jit(solution)/shard_map/all_to_all | solution.py:124
  45.3 0.1 fusion.233
  45.5 0.2 copy.122
  45.7 0.8 copy.124
  46.5 0.8 copy.120
  47.3 5.3 %fusion.31 = f32[7,18,3,16]{3,2,1,0:T(4,128)S(1)} fusion(s32[16]{0:T(128)S(1)} %get-tuple-element.25, s32[7,18,16]{2,1,0:T(8,128)S(1)} %copy.98, f32[7,18,16]{2,1,0:T(8,128)S(1)} %copy.97, s32[7,18,16]{2,1,0:T(8,128)S(1)} %copy.96, s32[3]{0:T(128)S(1)} %copy-done.15), kind=kOutput, calls=%fused_computation.54 | convolution fusion | flops 1624896 | bytes 48460 | tf_op jit(solution)/shard_map/kisr,kisn->kirn/dot_general | solution.py:62
  52.7 0.1 fusion.234
  52.8 0.8 copy.121
  53.7 0.8 copy.123
  54.5 0.8 copy.125
  55.4 4.0 %all-to-all-done.1 = bf16[80,16,128]{0,1,2:T(8,128)(2,1)S(1)} async-done(((bf16[80,16,128]{0,1,2:T(8,128)(2,1)}), bf16[80,16,128]{0,1,2:T(8,128)(2,1)S(1)}, u32[]{:S(2)}, u32[]{:S(2)}) %all-to-all-start.1) | async-done | bytes 327712 | tf_op jit(solution)/shard_map/all_to_all | solution.py:124
  59.4 0.3 copy.95
  59.7 0.4 convert_element_type.115
  60.2 0.5 reshape.122
  60.7 1.5 %fusion.230 = (f32[640,18,16]{0,2,1:T(8,128)}, f32[640,18,16]{0,2,1:T(8,128)}, f32[640,18,16]{0,2,1:T(8,128)}) fusion(f32[640,20,16]{0,2,1:T(8,128)S(1)} %pad_convert_fusion), kind=kLoop, calls=%fused_computation.294 | loop fusion | bytes 4423680 | tf_op jit(solution)/shard_map/slice | solution.py:72
  62.1 0.6 fusion.232
  62.8 0.7 pad_maximum_fusion
  63.5 0.6 reshape.123
  64.2 0.2 fusion.231
  64.3 0.9 copy-done.2
  65.2 0.2 copy-done.3
  65.4 0.2 copy-done.4
  65.8 2.9 %fusion.228 = (bf16[7,640,18,16]{1,0,3,2:T(8,128)(2,1)S(1)}, f32[7,640,18,16]{1,0,3,2:T(8,128)S(1)}) fusion(f32[7,18,16]{0,2,1:T(8,128)S(1)} %bitcast.155, f32[640,18,16]{0,2,1:T(8,128)S(1)} %get-tuple-element.13, f32[7,18,16]{0,2,1:T(8,128)S(1)} %bitcast.151, f32[640,18,16]{0,2,1:T(8,128)S(1)} %copy-done.3, f32[7,18,16]{0,2,1:T(8,128)S(1)} %bitcast.154, ...), kind=kLoop, calls=%fused_computation.292 | loop fusion | flops 15482880 | bytes 12213504 | tf_op jit(solution)/shard_map/convert.14
  68.7 1.3 collective-permute-start
  70.1 1.3 collective-permute-start.1
  71.4 2.0 %collective-permute-done.1 = bf16[7,640,1,16]{1,0,3,2:T(8,128)(2,1)S(1)} collective-permute-done((bf16[7,640,1,16]{1,0,3,2:T(8,128)(2,1)S(1)}, bf16[7,640,1,16]{1,0,3,2:T(8,128)(2,1)S(1)}, u32[]{:S(2)}, u32[]{:S(2)}) %collective-permute-start.1) | collective-permute-done | bytes 143392 | tf_op jit(solution)/shard_map/ppermute | solution.py:20
  73.5 0.4 fusion.1
  73.9 0.4 copy.128
  74.2 1.3 slice-done
  75.5 0.5 slice-done.1
  76.0 2.0 %convolution_convert_fusion.2 = bf16[256,640]{1,0:T(8,128)(2,1)S(1)} fusion(bf16[4480,256]{0,1:T(8,128)(2,1)S(1)} %bitcast.145, bf16[4480,640]{1,0:T(8,128)(2,1)S(1)} %bitcast.159), kind=kOutput, calls=%fused_computation.45 | convolution fusion | flops 1468170240 | bytes 8355840 | tf_op jit(solution)/shard_map/dot_general | solution.py:129
  78.0 2.7 %copy.111 = bf16[640,16,16]{2,1,0:T(8,128)(2,1)} copy(bf16[640,16,16]{0,2,1:T(8,128)(2,1)S(1)} %bitcast.156) | data formatting | bytes 655360 | tf_op jit(solution)/shard_map/convert_element_type | solution.py:137
  80.7 5.1 %reshape.135 = bf16[8,2,10240]{2,1,0:T(2,128)(2,1)} reshape(bf16[640,16,16]{2,1,0:T(8,128)(2,1)} %copy.111) | data formatting | bytes 655360
  85.8 4.0 %all-to-all-start.2 = ((bf16[8,2,10240]{2,1,0:T(2,128)(2,1)}), bf16[8,2,10240]{2,1,0:T(2,128)(2,1)S(1)}, u32[]{:S(2)}, u32[]{:S(2)}) async-start(bf16[8,2,10240]{2,1,0:T(2,128)(2,1)} %reshape.135), calls=%async_computation.2 | async-start | bytes 655360 | tf_op jit(solution)/shard_map/all_to_all | solution.py:136
  89.7 10.6 %all-to-all-done.2 = bf16[8,2,10240]{2,1,0:T(2,128)(2,1)S(1)} async-done(((bf16[8,2,10240]{2,1,0:T(2,128)(2,1)}), bf16[8,2,10240]{2,1,0:T(2,128)(2,1)S(1)}, u32[]{:S(2)}, u32[]{:S(2)}) %all-to-all-start.2) | async-done | bytes 327712 | tf_op jit(solution)/shard_map/all_to_all | solution.py:136
  100.3 2.9 %reshape.136 = bf16[640,16,16]{2,1,0:T(8,128)(2,1)} reshape(bf16[8,2,10240]{2,1,0:T(2,128)(2,1)S(1)} %all-to-all-done.2) | data formatting | bytes 655360
  103.2 3.0 %copy.113 = bf16[80,16,8,16]{0,3,2,1:T(8,128)(2,1)S(1)} copy(bf16[80,16,8,16]{3,1,0,2:T(8,128)(2,1)} %bitcast.144) | data formatting | bytes 655360 | tf_op jit(solution)/shard_map/all_to_all | solution.py:136
  106.2 0.3 copy.114
  106.5 1.0 convolution_convert_fusion.1
  107.6 0.6 copy.115
  108.1 18.0 %all_to_all.48 = bf16[80,16,128]{0,1,2:T(8,128)(2,1)S(1)} all-to-all(bf16[80,16,128]{0,1,2:T(8,128)(2,1)S(1)} %copy.115), channel_id=1, replica_groups=mesh['member'=2,'lon'=8,'lat'=2] {'lon'}, dimensions={2} | all-to-all | bytes 655360 | tf_op jit(solution)/shard_map/all_to_all | solution.py:147
  126.1 0.1 copy.116
  126.3 0.1 convert_bitcast_fusion
  126.4 0.3 copy.117
  126.7 0.3 reshape.129
  127.1 1.2 reshape.128
  128.3 1.2 fusion.95
  129.5 1.2 multiply_reduce_fusion
  130.9 6.0 %fusion.22 = bf16[640,256]{0,1:T(8,128)(2,1)} fusion(f32[640,256]{0,1:T(8,128)S(1)} %bitcast_add_fusion, bf16[1280,640]{1,0:T(8,128)(2,1)S(1)} %copy-done, bf16[640,1280]{1,0:T(8,128)(2,1)} %param.15, f32[640]{0:T(1024)S(1)} %copy-done.14, f32[256]{0:T(256)S(1)} %rsqrt.11, f32[256]{0:T(256)S(1)} %div.44), kind=kOutput, calls=%fused_computation.43 | convolution fusion | flops 861143040 | bytes 4264448 | tf_op jit(solution)/shard_map/dot_general | solution.py:163
  (48 shorter events, 0.8 us)
Async XLA Ops:
  0.0 130.9 %copy-start = (bf16[1280,640]{1,0:T(8,128)(2,1)S(1)}, bf16[1280,640]{1,0:T(8,128)(2,1)}, u32[]{:S(2)}) copy-start(bf16[1280,640]{1,0:T(8,128)(2,1)} %param.16) | copy-start | bytes 4915204
  3.7 12.5 %copy-start.11 = (s32[7,32,16]{1,2,0:T(8,128)S(1)}, s32[7,32,16]{1,2,0:T(8,128)}, u32[]{:S(2)}) copy-start(s32[7,32,16]{1,2,0:T(8,128)} %param.11) | copy-start | bytes 43012
  3.7 12.5 %copy-start.12 = (s32[7,32,16]{1,2,0:T(8,128)S(1)}, s32[7,32,16]{1,2,0:T(8,128)}, u32[]{:S(2)}) copy-start(s32[7,32,16]{1,2,0:T(8,128)} %param.10) | copy-start | bytes 43012
  3.7 12.9 %copy-start.13 = (f32[7,32,16]{1,2,0:T(8,128)S(1)}, f32[7,32,16]{1,2,0:T(8,128)}, u32[]{:S(2)}) copy-start(f32[7,32,16]{1,2,0:T(8,128)} %param.12) | copy-start | bytes 43012
  8.8 8.1 %copy-start.15 = (s32[3]{0:T(128)S(1)}, s32[3]{0:T(128)}, u32[]{:S(2)}) copy-start(s32[3]{0:T(128)} %constant.173.clone) | copy-start | bytes 40
  8.8 17.7 %all-to-all-start = ((bf16[8,2,10240]{2,1,0:T(2,128)(2,1)}), bf16[8,2,10240]{2,1,0:T(2,128)(2,1)S(1)}, u32[]{:S(2)}, u32[]{:S(2)}) async-start(bf16[8,2,10240]{2,1,0:T(2,128)(2,1)} %reshape.133), calls=%async_computation | async-start | bytes 655360 | tf_op jit(solution)/shard_map/all_to_all | solution.py:112
  41.7 17.7 %all-to-all-start.1 = ((bf16[80,16,128]{0,1,2:T(8,128)(2,1)}), bf16[80,16,128]{0,1,2:T(8,128)(2,1)S(1)}, u32[]{:S(2)}, u32[]{:S(2)}) async-start(bf16[80,16,128]{0,1,2:T(8,128)(2,1)} %copy.93), calls=%async_computation.1 | async-start | bytes 1048576 | tf_op jit(solution)/shard_map/all_to_all | solution.py:124
  64.1 1.1 copy-start.2
  64.1 1.3 copy-start.3
  64.1 1.5 %copy-start.4 = (f32[640,18,16]{0,2,1:T(8,128)S(1)}, f32[640,18,16]{0,2,1:T(8,128)}, u32[]{:S(2)}) copy-start(f32[640,18,16]{0,2,1:T(8,128)} %get-tuple-element.11) | copy-start | bytes 2211844
  64.1 1.5 %copy-start.6 = (f32[7,18,1,16]{0,3,1,2:T(8,128)S(1)}, f32[7,18,1,16]{0,3,1,2:T(8,128)}, u32[]{:S(2)}) copy-start(f32[7,18,1,16]{0,3,1,2:T(8,128)} %copy.124) | copy-start | bytes 24196
  64.1 1.6 %copy-start.7 = (f32[7,18,1,16]{0,3,1,2:T(8,128)S(1)}, f32[7,18,1,16]{0,3,1,2:T(8,128)}, u32[]{:S(2)}) copy-start(f32[7,18,1,16]{0,3,1,2:T(8,128)} %copy.120) | copy-start | bytes 24196
  64.1 1.6 %copy-start.8 = (f32[7,18,1,16]{0,3,1,2:T(8,128)S(1)}, f32[7,18,1,16]{0,3,1,2:T(8,128)}, u32[]{:S(2)}) copy-start(f32[7,18,1,16]{0,3,1,2:T(8,128)} %copy.121) | copy-start | bytes 24196
  64.1 1.7 %copy-start.9 = (f32[7,18,1,16]{0,3,1,2:T(8,128)S(1)}, f32[7,18,1,16]{0,3,1,2:T(8,128)}, u32[]{:S(2)}) copy-start(f32[7,18,1,16]{0,3,1,2:T(8,128)} %copy.123) | copy-start | bytes 24196
  64.2 1.7 %copy-start.10 = (f32[7,18,1,16]{0,3,1,2:T(8,128)S(1)}, f32[7,18,1,16]{0,3,1,2:T(8,128)}, u32[]{:S(2)}) copy-start(f32[7,18,1,16]{0,3,1,2:T(8,128)} %copy.125) | copy-start | bytes 24196
  68.7 2.6 %collective-permute-start = (bf16[7,640,1,16]{1,0,3,2:T(8,128)(2,1)S(1)}, bf16[7,640,1,16]{1,0,3,2:T(8,128)(2,1)S(1)}, u32[]{:S(2)}, u32[]{:S(2)}) collective-permute-start(bf16[7,640,1,16]{1,0,3,2:T(8,128)(2,1)S(1)} %get-tuple-element.7), channel_id=1, source_target_pairs={{0,1},{2,3},{4,5},{6,7},{8,9},{10,11},{12,13},{14,15},{16,17},{18,... | collective-permute-start | bytes 430088 | tf_op jit(solution)/shard_map/ppermute | solution.py:17
  70.1 3.3 %collective-permute-start.1 = (bf16[7,640,1,16]{1,0,3,2:T(8,128)(2,1)S(1)}, bf16[7,640,1,16]{1,0,3,2:T(8,128)(2,1)S(1)}, u32[]{:S(2)}, u32[]{:S(2)}) collective-permute-start(bf16[7,640,1,16]{1,0,3,2:T(8,128)(2,1)S(1)} %get-tuple-element.8), channel_id=1, source_target_pairs={{1,0},{3,2},{5,4},{7,6},{9,8},{11,10},{13,12},{15,14},{17,16},{19,... | collective-permute-start | bytes 430088 | tf_op jit(solution)/shard_map/ppermute | solution.py:20
  73.3 2.2 %slice-start = ((s8[5734400]{0:T(1024)(128)(4,1)}), s8[4194304]{0:T(1024)(128)(4,1)S(1)}, s32[]{:S(2)}) async-start(s8[5734400]{0:T(1024)(128)(4,1)} %bitcast.157), calls=%async_computation.4 | async-start | bytes 8388608
  73.4 2.6 %slice-start.1 = ((s8[5734400]{0:T(1024)(128)(4,1)}), s8[1540096]{0:T(1024)(128)(4,1)S(1)}, s32[]{:S(2)}) async-start(s8[5734400]{0:T(1024)(128)(4,1)} %bitcast.157), calls=%async_computation.5 | async-start | bytes 3080192
  85.8 14.5 %all-to-all-start.2 = ((bf16[8,2,10240]{2,1,0:T(2,128)(2,1)}), bf16[8,2,10240]{2,1,0:T(2,128)(2,1)S(1)}, u32[]{:S(2)}, u32[]{:S(2)}) async-start(bf16[8,2,10240]{2,1,0:T(2,128)(2,1)} %reshape.135), calls=%async_computation.2 | async-start | bytes 655360 | tf_op jit(solution)/shard_map/all_to_all | solution.py:136
  128.3 2.6 %copy-start.1 = (bf16[640,16,16]{0,2,1:T(8,128)(2,1)S(1)}, bf16[640,16,16]{0,2,1:T(8,128)(2,1)}, u32[]{:S(2)}) copy-start(bf16[640,16,16]{0,2,1:T(8,128)(2,1)} %param.9) | copy-start | bytes 983044
  128.3 2.6 %copy-start.5 = (f32[640,256]{0,1:T(8,128)S(1)}, f32[640,256]{0,1:T(8,128)}, u32[]{:S(2)}) copy-start(f32[640,256]{0,1:T(8,128)} %reshape.128) | copy-start | bytes 1966084
  129.5 1.5 %copy-start.14 = (f32[640]{0:T(1024)S(1)}, f32[640]{0:T(1024)}, u32[]{:S(2)}) copy-start(f32[640]{0:T(1024)} %param.14) | copy-start | bytes 7684
where the time goes:
time: 138 us; the launch traced here: 137 us
  local copies, waits for them, and re-layouts  52.1 us (38%)
  waiting for transfers between devices  20.9 us (15%)
  matrix products  20.5 us (15%)
  blocking collectives  18 us (13%)
  starting transfers between devices  17.6 us (13%)
  other arithmetic  7.37 us (5%)
    unnamed x42, local copies, waits for them, and re-layouts  23.4 us
    all_to_all x1, blocking collectives, on_device(): lax.all_to_all(spatial.astype(jnp.bfloat16), 'lon', split_axis=2, concat_...  18 us
    all_to_all x1, waiting for transfers between devices, on_device(): lax.all_to_all(mixed_spec.astype(jnp.bfloat16), 'lon', split_axis=0, conc...  10.6 us
    all_to_all x1, starting transfers between devices, on_device(): lax.all_to_all(fields, 'lon', split_axis=0, concat_axis=2, tiled=True)  7.41 us
    all_to_all x1, local copies, waits for them, and re-layouts, on_device(): lax.all_to_all(fields, 'lon', split_axis=0, concat_axis=2, tiled=True)  6.32 us
    dot_general x1, matrix products, on_device(): lax.dot_general(down_weight, hidden, (((0,), (0,)), ((), ())), preferred_...  5.95 us
    dot_general x1, matrix products, filter_spectra(): jnp.einsum('kisr,kisn->kirn', picked, jnp.sin(sin_angle), precision=lax.P...  5.33 us
    dot_general x1, matrix products, filter_spectra(): jnp.einsum('kisr,kisn->kirn', picked, jnp.cos(cos_angle), precision=lax.P...  5.32 us
  transfers between devices with their start and end apart: 5, of which 4 were waited for; matrix products, arithmetic and copies ran while one was open for 12% of the time, Pallas kernels for 0%

commit v1 on v0

v1 whole, which is shorter than its diff:
```python
import functools
import math

import jax
import jax.numpy as jnp
from jax import lax
from jax.experimental import pallas as pl
from jax.experimental.pallas import tpu as pltpu
from jax.sharding import PartitionSpec as P

norm_eps = 1e-05
MESH = pl.DeviceIdType.MESH


def plan_copies(lon_count, lat_count, rows, cols):
    lon_total, row_total = lon_count * cols, lat_count * rows

    def distance(row):
        nearest = min(row + 1, row_total - row)
        reach = min(lon_total // 2, 4 * row_total // nearest)
        return min(-(-reach // cols), lon_count // 2)

    need = [distance(max(p - 1, 0)) for p in range(rows)]
    split = rows // 2 - 1
    early, late = [], []
    for delta in range(-(lon_count // 2) + 1, lon_count // 2 + 1):
        if delta == 0:
            continue
        count = sum(1 for d in need if d >= abs(delta))
        if count > split:
            early.append(("block", delta, split, count))
        if min(count, split) > 0:
            late.append(("block", delta, 0, min(count, split)))
    edge = 0
    for boundary in range(1, lat_count):
        edge = max(edge, distance(boundary * rows - 1), distance(boundary * rows))
    halo = []
    if lat_count > 1:
        for delta in range(-(lon_count // 2) + 1, lon_count // 2 + 1):
            if abs(delta) <= edge:
                halo.append(("down", delta, 0, 1))
                halo.append(("up", delta, 0, 1))
    late.sort(key=lambda item: -abs(item[1]))
    return halo + early, late


def block_kernel(
    lon_count,
    lat_count,
    early,
    late,
    x_ref,
    rows_ref,
    lons_ref,
    weights_ref,
    gain_ref,
    mix_hbm,
    up_hbm,
    down_hbm,
    out_ref,
    window,
    filters,
    product,
    mix_ref,
    up_ref,
    down_ref,
    send_sem,
    recv_sem,
    load_sem,
):
    rows, cols, channels = x_ref.shape
    bases = mix_ref.shape[0] // channels
    entries = rows_ref.shape[2]
    lon_total = lon_count * cols
    middle = lon_count // 2
    half = rows // 2
    me, lat = lax.axis_index("lon"), lax.axis_index("lat")
    north = 2 * lat < lat_count
    has_low, has_high = lat > 0, lat < lat_count - 1

    loads = [
        pltpu.make_async_copy(mix_hbm, mix_ref, load_sem.at[0]),
        pltpu.make_async_copy(up_hbm, up_ref, load_sem.at[1]),
        pltpu.make_async_copy(down_hbm, down_ref, load_sem.at[2]),
    ]
    for load in loads:
        load.start()

    window[...] = jnp.zeros_like(window)
    window[1 : rows + 1, middle * cols : (middle + 1) * cols, :] = x_ref[...]

    barrier = pltpu.get_barrier_semaphore()
    halo_deltas = [item[1] for item in early if item[0] == "down"]
    for delta in range(1, lon_count):
        pl.semaphore_signal(
            barrier, inc=1, device_id={"lon": lax.rem(me + delta, lon_count)}, device_id_type=MESH
        )
    for present, other in ((has_low, lat - 1), (has_high, lat + 1)):

        @pl.when(present)
        def _():
            for delta in halo_deltas:
                target = lax.rem(me + lon_count - delta, lon_count)
                pl.semaphore_signal(
                    barrier, inc=1, device_id={"lon": target, "lat": other}, device_id_type=MESH
                )

    sides = jnp.where(has_low, 1, 0) + jnp.where(has_high, 1, 0)
    pl.semaphore_wait(barrier, lon_count - 1 + sides * len(halo_deltas))

    def copy_of(index, item):
        kind, delta, first, last = item
        target = lax.rem(me + lon_count - delta, lon_count)
        slot = (delta + middle) % lon_count
        if kind == "block":
            start = jnp.where(north, first, rows - last)
            source = x_ref.at[pl.ds(start, last - first)]
            landing = window.at[pl.ds(start + 1, last - first), pl.ds(slot * cols, cols)]
            device = {"lon": target}
        elif kind == "down":
            source = x_ref.at[pl.ds(rows - 1, 1)]
            landing = window.at[pl.ds(0, 1), pl.ds(slot * cols, cols)]
            device = {"lon": target, "lat": jnp.minimum(lat + 1, lat_count - 1)}
        else:
            source = x_ref.at[pl.ds(0, 1)]
            landing = window.at[pl.ds(rows + 1, 1), pl.ds(slot * cols, cols)]
            device = {"lon": target, "lat": jnp.maximum(lat - 1, 0)}
        return pltpu.make_async_remote_copy(
            src_ref=source,
            dst_ref=landing,
            send_sem=send_sem.at[index],
            recv_sem=recv_sem.at[index],
            device_id=device,
            device_id_type=MESH,
        )

    copies = list(enumerate(early + late))

    def each(items, sending, action):
        for index, item in items:
            if item[0] == "block":
                action(copy_of(index, item))
            else:
                present = has_high if (item[0] == "down") == sending else has_low

                @pl.when(present)
                def _():
                    action(copy_of(index, item))

    each(copies, True, lambda copy: copy.start())

    first_row = pl.multiple_of(lat * rows, rows)
    lanes = lax.broadcasted_iota(jnp.int32, (rows, lon_total), 1)

    def build(k, carry):
        spot = lons_ref[k, pl.ds(first_row, rows), :] + middle * cols
        spot = jnp.where(spot >= lon_total, spot - lon_total, spot)
        row_offset = rows_ref[k, pl.ds(first_row, rows), :]
        weight = weights_ref[k, pl.ds(first_row, rows), :]
        picked = [jnp.where(row_offset == r, weight, 0.0) for r in (-1, 0, 1)]
        sums = [jnp.zeros((rows, lon_total), jnp.float32) for _ in range(3)]
        for s in range(entries):
            hit = spot[:, s : s + 1] == lanes
            for r in range(3):
                sums[r] = sums[r] + jnp.where(hit, picked[r][:, s : s + 1], 0.0)
        for r in range(3):
            for i in range(rows):
                line = jnp.broadcast_to(sums[r][i : i + 1, :], (cols, lon_total))
                turned = pltpu.roll(line, 0, 1, stride=1, stride_axis=0)
                filters[i, pl.ds(pl.multiple_of(k * cols, cols), cols),
                        r * lon_total : (r + 1) * lon_total] = turned.astype(jnp.bfloat16)
        return carry

    lax.fori_loop(0, bases, build, 0)

    def group(start):
        def filter_row(t, carry):
            i = start + t
            source = window[pl.ds(i, 3)].reshape(3 * lon_total, channels)
            filtered = jnp.dot(filters[i], source, preferred_element_type=jnp.float32)
            filtered = filtered.astype(jnp.bfloat16)
            at = pl.multiple_of(t * cols, cols)
            for k in range(bases):
                product[pl.ds(at, cols), k * channels : (k + 1) * channels] = filtered[
                    k * cols : (k + 1) * cols
                ]
            return carry

        lax.fori_loop(0, half, filter_row, 0)
        mixed = jnp.dot(product[...], mix_ref[...], preferred_element_type=jnp.float32)
        own = x_ref[pl.ds(start, half)].reshape(half * cols, channels)
        latent = own.astype(jnp.float32) + mixed
        mean = jnp.mean(latent, axis=1, keepdims=True)
        centred = latent - mean
        variance = jnp.mean(centred * centred, axis=1, keepdims=True)
        normed = (centred * lax.rsqrt(variance + norm_eps) * gain_ref[...]).astype(jnp.bfloat16)
        raised = jnp.dot(normed, up_ref[...], preferred_element_type=jnp.float32)
        hidden = 0.5 * raised * (1.0 + lax.erf(raised * math.sqrt(0.5)))
        lowered = jnp.dot(
            hidden.astype(jnp.bfloat16), down_ref[...], preferred_element_type=jnp.float32
        )
        result = (latent + lowered).astype(jnp.bfloat16)
        out_ref[pl.ds(start, half)] = result.reshape(half, cols, channels)

    each(copies[: len(early)], False, lambda copy: copy.wait_recv())
    loads[0].wait()
    loads[1].wait()
    loads[2].wait()
    group(jnp.where(north, half, 0))
    each(copies[len(early) :], False, lambda copy: copy.wait_recv())
    group(jnp.where(north, 0, half))
    each(copies, True, lambda copy: copy.wait_send())


def on_device(
    lon_count,
    lat_count,
    fields,
    support_rows,
    support_lons,
    support_weights,
    mix_weight,
    norm_gain,
    up_weight,
    down_weight,
):
    channels, rows, cols = fields.shape
    bases, hidden = mix_weight.shape[0], up_weight.shape[1]
    lon_total = lon_count * cols
    early, late = plan_copies(lon_count, lat_count, rows, cols)
    count = len(early) + len(late)
    in_vmem = pl.BlockSpec(memory_space=pltpu.VMEM)
    anywhere = pl.BlockSpec(memory_space=pl.ANY)
    result = pl.pallas_call(
        functools.partial(block_kernel, lon_count, lat_count, early, late),
        out_shape=jax.ShapeDtypeStruct((rows, cols, channels), jnp.bfloat16),
        in_specs=[in_vmem] * 5 + [anywhere] * 3,
        out_specs=in_vmem,
        scratch_shapes=[
            pltpu.VMEM((rows + 2, lon_total, channels), jnp.bfloat16),
            pltpu.VMEM((rows, bases * cols, 3 * lon_total), jnp.bfloat16),
            pltpu.VMEM((rows // 2 * cols, bases * channels), jnp.bfloat16),
            pltpu.VMEM((bases * channels, channels), jnp.bfloat16),
            pltpu.VMEM((channels, hidden), jnp.bfloat16),
            pltpu.VMEM((hidden, channels), jnp.bfloat16),
            pltpu.SemaphoreType.DMA((count,)),
            pltpu.SemaphoreType.DMA((count,)),
            pltpu.SemaphoreType.DMA((3,)),
        ],
        compiler_params=pltpu.CompilerParams(
            collective_id=0, has_side_effects=True, vmem_limit_bytes=56 * 1024 * 1024
        ),
    )(
        jnp.transpose(fields, (1, 2, 0)),
        support_rows,
        support_lons,
        support_weights,
        norm_gain.reshape(1, channels),
        mix_weight.reshape(bases * channels, channels),
        up_weight,
        down_weight,
    )
    return jnp.transpose(result, (2, 0, 1))


def solution(mesh):
    in_specs = (P("member", "lat", "lon"), P(), P(), P(), P(), P(), P(), P())
    out_specs = P("member", "lat", "lon")
    return jax.shard_map(
        functools.partial(on_device, mesh.shape["lon"], mesh.shape["lat"]),
        mesh=mesh,
        in_specs=in_specs,
        out_specs=out_specs,
        check_vma=False,
    )
```

time: 138 us -> 41.5 us (0.30)
  local copies, waits for them, and re-layouts: 52.1 us -> 7.69 us
  Pallas kernels: 0 us -> 33.5 us
  waiting for transfers between devices: 20.9 us -> 0 us
  matrix products: 20.5 us -> 0 us
  blocking collectives: 18 us -> 0 us
  starting transfers between devices: 17.6 us -> 0 us
  other arithmetic: 7.37 us -> 0 us
    pallas_call x0 -> x1, Pallas kernels: none -> 33.5 us  [on_device(): pl.pallas_call(functools.partial(block_kernel, lon_count, lat_count, earl...]
    dot_general x6 -> x0, matrix products: 20.5 us -> none  [the longest x1 5.95 us: on_device(): lax.dot_general(down_weight, hidden, (((0,), (0,)), ((), ())), preferred_...]
    all_to_all x3 -> x0, waiting for transfers between devices: 18.9 us -> none  [the longest x1 10.6 us: on_device(): lax.all_to_all(mixed_spec.astype(jnp.bfloat16), 'lon', split_axis=0, conc...]
    all_to_all x1 -> x0, blocking collectives: 18 us -> none  [on_device(): lax.all_to_all(spatial.astype(jnp.bfloat16), 'lon', split_axis=2, concat_...]
    unnamed x42 -> x4, local copies, waits for them, and re-layouts: 23.4 us -> 6.41 us
    all_to_all x3 -> x0, starting transfers between devices: 15 us -> none  [the longest x1 7.41 us: on_device(): lax.all_to_all(fields, 'lon', split_axis=0, concat_axis=2, tiled=True)]
    all_to_all x3 -> x0, local copies, waits for them, and re-layouts: 9.42 us -> none  [the longest x1 6.32 us: on_device(): lax.all_to_all(fields, 'lon', split_axis=0, concat_axis=2, tiled=True)]
    convert_element_type x9 -> x0, local copies, waits for them, and re-layouts: 7.41 us -> none  [the longest x1 2.69 us: on_device(): mixed_spec.astype(jnp.bfloat16)]
  transfers between devices with their start and end apart: 5 -> 0, of which waited for: 4 -> 0; matrix products, arithmetic and copies ran while one was open for 12% -> 0% of each run, Pallas kernels for 0% -> 0%
where the time goes in v1:
time: 41.5 us; the launch traced here: 41.2 us
  Pallas kernels  33.5 us (81%)
  local copies, waits for them, and re-layouts  7.69 us (19%)
    pallas_call x1, Pallas kernels, on_device(): pl.pallas_call(functools.partial(block_kernel, lon_count, lat_count, earl...  33.5 us
    unnamed x4, local copies, waits for them, and re-layouts  6.41 us
    reshape x1, local copies, waits for them, and re-layouts, on_device(): norm_gain.reshape(1, channels)  1.28 us

profile of v1, /device:TPU:0, one launch (start us, length us, event | category | flops | bytes accessed | tf_op | source)
XLA Modules:
  0.0 41.2 jit_solution(12728218372642389986)
XLA Ops:
  0.0 1.3 %reshape.6.gain_ref = f32[1,640]{1,0:T(1,128)} reshape(f32[640]{0:T(1024)} %param.13) | data formatting | bytes 5120 | tf_op jit(solution)/shard_map/reshape | solution.py:258
  1.3 1.6 %copy.9.rows_ref = s32[7,32,16]{2,1,0:T(8,128)} copy(s32[7,32,16]{1,2,0:T(8,128)} %param.9) | data formatting | bytes 28672 | tf_op args[1]
  2.8 1.6 %copy.10.lons_ref = s32[7,32,16]{2,1,0:T(8,128)} copy(s32[7,32,16]{1,2,0:T(8,128)} %param.10) | data formatting | bytes 28672 | tf_op args[2]
  4.4 1.6 %copy.11.weights_ref = f32[7,32,16]{2,1,0:T(8,128)} copy(f32[7,32,16]{1,2,0:T(8,128)} %param.11) | data formatting | bytes 28672 | tf_op args[3]
  6.0 33.5 %shard_map.82 = bf16[16,16,640]{2,1,0:T(8,128)(2,1)} custom-call(bf16[16,16,640]{2,1,0:T(8,128)(2,1)} %bitcast.5, s32[7,32,16]{2,1,0:T(8,128)} %copy.9.rows_ref, s32[7,32,16]{2,1,0:T(8,128)} %copy.10.lons_ref, f32[7,32,16]{2,1,0:T(8,128)} %copy.11.weights_ref, f32[1,640]{1,0:T(1,128)} %reshape.6.gain_ref, bf16[4480,640]{1,0:T(8,128)(2,1)} %bitcast.3, ...), custom_call_target="tpu_custom_call" | custom-call | tf_op jit(solution)/shard_map/pallas_call | solution.py:234
  39.5 1.7 %copy.13 = bf16[640,16,16]{0,2,1:T(8,128)(2,1)} copy(bf16[640,16,16]{0,2,1:T(8,128)(2,1)} %bitcast.4) | data formatting | bytes 655360

commit v2 on v1

--- a/solution.py
+++ b/solution.py
@@ -21,34 +21,32 @@
         return min(-(-reach // cols), lon_count // 2)
 
     need = [distance(max(p - 1, 0)) for p in range(rows)]
-    split = rows // 2 - 1
-    early, late = [], []
-    for delta in range(-(lon_count // 2) + 1, lon_count // 2 + 1):
-        if delta == 0:
-            continue
-        count = sum(1 for d in need if d >= abs(delta))
-        if count > split:
-            early.append(("block", delta, split, count))
-        if min(count, split) > 0:
-            late.append(("block", delta, 0, min(count, split)))
+    deltas = [d for d in range(1 - lon_count // 2, lon_count // 2 + 1) if d != 0]
+    counts = {delta: sum(1 for d in need if d >= abs(delta)) for delta in deltas}
     edge = 0
     for boundary in range(1, lat_count):
         edge = max(edge, distance(boundary * rows - 1), distance(boundary * rows))
-    halo = []
+    halo = [d for d in range(1 - lon_count // 2, lon_count // 2 + 1) if abs(d) <= edge]
+    groups = [(rows // 2, rows), (rows // 4, rows // 2), (0, rows // 4)]
+    stages = []
+    upper = rows
+    for low, _ in groups:
+        lower = max(low - 1, 0)
+        stage = []
+        for delta in sorted(deltas, key=lambda d: -abs(d)):
+            if min(counts[delta], upper) > lower:
+                stage.append(("block", delta, lower, min(counts[delta], upper)))
+        stages.append(stage)
+        upper = lower
     if lat_count > 1:
-        for delta in range(-(lon_count // 2) + 1, lon_count // 2 + 1):
-            if abs(delta) <= edge:
-                halo.append(("down", delta, 0, 1))
-                halo.append(("up", delta, 0, 1))
-    late.sort(key=lambda item: -abs(item[1]))
-    return halo + early, late
+        stages[0] = [(side, d, 0, 1) for d in halo for side in ("down", "up")] + stages[0]
+    return groups, stages, counts, halo
 
 
 def block_kernel(
     lon_count,
     lat_count,
-    early,
-    late,
+    plan,
     x_ref,
     rows_ref,
     lons_ref,
@@ -69,11 +67,10 @@
     load_sem,
 ):
     rows, cols, channels = x_ref.shape
-    bases = mix_ref.shape[0] // channels
-    entries = rows_ref.shape[2]
+    bases, entries = rows_ref.shape[:2]
     lon_total = lon_count * cols
     middle = lon_count // 2
-    half = rows // 2
+    groups, stages, counts, halo = plan
     me, lat = lax.axis_index("lon"), lax.axis_index("lat")
     north = 2 * lat < lat_count
     has_low, has_high = lat > 0, lat < lat_count - 1
@@ -86,11 +83,8 @@
     for load in loads:
         load.start()
 
-    window[...] = jnp.zeros_like(window)
-    window[1 : rows + 1, middle * cols : (middle + 1) * cols, :] = x_ref[...]
-
     barrier = pltpu.get_barrier_semaphore()
-    halo_deltas = [item[1] for item in early if item[0] == "down"]
+    halo_deltas = halo if lat_count > 1 else []
     for delta in range(1, lon_count):
         pl.semaphore_signal(
             barrier, inc=1, device_id={"lon": lax.rem(me + delta, lon_count)}, device_id_type=MESH
@@ -134,7 +128,9 @@
             device_id_type=MESH,
         )
 
-    copies = list(enumerate(early + late))
+    copies = []
+    for stage in stages:
+        copies.append(list(enumerate(stage, sum(len(done) for done in copies))))
 
     def each(items, sending, action):
         for index, item in items:
@@ -147,17 +143,52 @@
                 def _():
                     action(copy_of(index, item))
 
-    each(copies, True, lambda copy: copy.start())
-
-    first_row = pl.multiple_of(lat * rows, rows)
+    for stage in copies:
+        each(stage, True, lambda copy: copy.start())
+
+    window[1 : rows + 1, middle * cols : (middle + 1) * cols, :] = x_ref[...]
+    for delta, count in counts.items():
+        slot = (delta + middle) % lon_count
+        if count < rows:
+            gap = (rows - count, cols, channels)
+            window[pl.ds(jnp.where(north, count, 0) + 1, rows - count),
+                   slot * cols : (slot + 1) * cols] = jnp.zeros(gap, jnp.bfloat16)
+    for present, line in ((has_low, 0), (has_high, rows + 1)):
+        for delta in range(1 - middle, middle + 1):
+            slot = (delta + middle) % lon_count
+
+            def clear():
+                window[line, slot * cols : (slot + 1) * cols] = jnp.zeros(
+                    (cols, channels), jnp.bfloat16
+                )
+
+            if delta in halo and lat_count > 1:
+                pl.when(jnp.logical_not(present))(clear)
+            else:
+                clear()
+
     lanes = lax.broadcasted_iota(jnp.int32, (rows, lon_total), 1)
+    wide = (rows, rows_ref.shape[2])
+    own_rows = (
+        lax.broadcasted_iota(jnp.int32, wide, 0) + lat * rows
+        == lax.broadcasted_iota(jnp.int32, wide, 1)
+    ).astype(jnp.float32)
+
+    def own(ref, k):
+        return lax.dot_general(
+            own_rows,
+            ref[k].astype(jnp.float32),
+            (((1,), (1,)), ((), ())),
+            precision=lax.Precision.HIGHEST,
+            preferred_element_type=jnp.float32,
+        )
 
     def build(k, carry):
-        spot = lons_ref[k, pl.ds(first_row, rows), :] + middle * cols
+        spot = own(lons_ref, k).astype(jnp.int32) + middle * cols
         spot = jnp.where(spot >= lon_total, spot - lon_total, spot)
-        row_offset = rows_ref[k, pl.ds(first_row, rows), :]
-        weight = weights_ref[k, pl.ds(first_row, rows), :]
-        picked = [jnp.where(row_offset == r, weight, 0.0) for r in (-1, 0, 1)]
+        row_offset = own(rows_ref, k)
+        weight = own(weights_ref, k)
+        picked = [jnp.where(row_offset == r, weight, 0.0) for r in (-1.0, 0.0, 1.0)]
         sums = [jnp.zeros((rows, lon_total), jnp.float32) for _ in range(3)]
         for s in range(entries):
             hit = spot[:, s : s + 1] == lanes
@@ -173,7 +204,10 @@
 
     lax.fori_loop(0, bases, build, 0)
 
-    def group(start):
+    def group(low, high):
+        start = jnp.where(north, low, rows - high)
+        half = high - low
+        lines = half * cols
         def filter_row(t, carry):
             i = start + t
             source = window[pl.ds(i, 3)].reshape(3 * lon_total, channels)
@@ -187,13 +221,13 @@
             return carry
 
         lax.fori_loop(0, half, filter_row, 0)
-        mixed = jnp.dot(product[...], mix_ref[...], preferred_element_type=jnp.float32)
-        own = x_ref[pl.ds(start, half)].reshape(half * cols, channels)
-        latent = own.astype(jnp.float32) + mixed
+        mixed = jnp.dot(product[:lines], mix_ref[...], preferred_element_type=jnp.float32)
+        here = x_ref[pl.ds(start, half)].reshape(lines, channels)
+        latent = here.astype(jnp.float32) + mixed
         mean = jnp.mean(latent, axis=1, keepdims=True)
         centred = latent - mean
         variance = jnp.mean(centred * centred, axis=1, keepdims=True)
-        normed = (centred * lax.rsqrt(variance + norm_eps) * gain_ref[...]).astype(jnp.bfloat16)
+        normed = (centred * lax.rsqrt(variance + norm_eps) * gain_ref[...][None, :]).astype(jnp.bfloat16)
         raised = jnp.dot(normed, up_ref[...], preferred_element_type=jnp.float32)
         hidden = 0.5 * raised * (1.0 + lax.erf(raised * math.sqrt(0.5)))
         lowered = jnp.dot(
@@ -202,14 +236,14 @@
         result = (latent + lowered).astype(jnp.bfloat16)
         out_ref[pl.ds(start, half)] = result.reshape(half, cols, channels)
 
-    each(copies[: len(early)], False, lambda copy: copy.wait_recv())
-    loads[0].wait()
-    loads[1].wait()
-    loads[2].wait()
-    group(jnp.where(north, half, 0))
-    each(copies[len(early) :], False, lambda copy: copy.wait_recv())
-    group(jnp.where(north, 0, half))
-    each(copies, True, lambda copy: copy.wait_send())
+    for stage, (low, high) in zip(copies, groups):
+        each(stage, False, lambda copy: copy.wait_recv())
+        if stage is copies[0]:
+            for load in loads:
+                load.wait()
+        group(low, high)
+    for stage in copies:
+        each(stage, True, lambda copy: copy.wait_send())
 
 
 def on_device(
@@ -227,12 +261,12 @@
     channels, rows, cols = fields.shape
     bases, hidden = mix_weight.shape[0], up_weight.shape[1]
     lon_total = lon_count * cols
-    early, late = plan_copies(lon_count, lat_count, rows, cols)
-    count = len(early) + len(late)
+    plan = plan_copies(lon_count, lat_count, rows, cols)
+    count = sum(len(stage) for stage in plan[1])
     in_vmem = pl.BlockSpec(memory_space=pltpu.VMEM)
     anywhere = pl.BlockSpec(memory_space=pl.ANY)
     result = pl.pallas_call(
-        functools.partial(block_kernel, lon_count, lat_count, early, late),
+        functools.partial(block_kernel, lon_count, lat_count, plan),
         out_shape=jax.ShapeDtypeStruct((rows, cols, channels), jnp.bfloat16),
         in_specs=[in_vmem] * 5 + [anywhere] * 3,
         out_specs=in_vmem,
@@ -252,10 +286,10 @@
         ),
     )(
         jnp.transpose(fields, (1, 2, 0)),
-        support_rows,
-        support_lons,
-        support_weights,
-        norm_gain.reshape(1, channels),
+        jnp.transpose(support_rows, (0, 2, 1)),
+        jnp.transpose(support_lons, (0, 2, 1)),
+        jnp.transpose(support_weights, (0, 2, 1)),
+        norm_gain,
         mix_weight.reshape(bases * channels, channels),
         up_weight,
         down_weight,

time: 41.5 us -> 34.5 us (0.83)
  local copies, waits for them, and re-layouts: 7.69 us -> 1.73 us
  Pallas kernels: 33.5 us -> 32.6 us
    unnamed x4 -> x1, local copies, waits for them, and re-layouts: 6.41 us -> 1.73 us
    reshape x1 -> x0, local copies, waits for them, and re-layouts: 1.28 us -> none  [on_device(): norm_gain.reshape(1, channels)]
    pallas_call x1, Pallas kernels: 33.5 us -> 32.6 us  [on_device(): pl.pallas_call(functools.partial(block_kernel, lon_count, lat_count, plan...]
where the time goes in v2:
time: 34.5 us; the launch traced here: 34.3 us
  Pallas kernels  32.6 us (94%)
  local copies, waits for them, and re-layouts  1.73 us (5%)
    pallas_call x1, Pallas kernels, on_device(): pl.pallas_call(functools.partial(block_kernel, lon_count, lat_count, plan...  32.6 us
    unnamed x1, local copies, waits for them, and re-layouts  1.73 us

profile of v2, /device:TPU:0, one launch (start us, length us, event | category | flops | bytes accessed | tf_op | source)
XLA Modules:
  0.0 34.3 jit_solution(6597812275300094129)
XLA Ops:
  0.0 32.6 %shard_map.82 = bf16[16,16,640]{2,1,0:T(8,128)(2,1)} custom-call(bf16[16,16,640]{2,1,0:T(8,128)(2,1)} %bitcast.8, s32[7,16,32]{2,1,0:T(8,128)} %bitcast.9, s32[7,16,32]{2,1,0:T(8,128)} %bitcast.10, f32[7,16,32]{2,1,0:T(8,128)} %bitcast.11, f32[640]{0:T(1024)} %gain_ref.1, bf16[4480,640]{1,0:T(8,128)(2,1)} %bitcast.6, bf16[640,1280]{1,0:T(8,128)(2,1)} %up_hbm.1, ...), custom_call_target="tpu_custom_call" | custom-call | tf_op jit(solution)/shard_map/pallas_call | solution.py:268
  32.6 1.7 %copy.10 = bf16[640,16,16]{0,2,1:T(8,128)(2,1)} copy(bf16[640,16,16]{0,2,1:T(8,128)(2,1)} %bitcast.7) | data formatting | bytes 655360

commit v3 on v2

--- a/solution.py
+++ b/solution.py
@@ -64,6 +64,7 @@
     down_ref,
     send_sem,
     recv_sem,
+    relay_sem,
     load_sem,
 ):
     rows, cols, channels = x_ref.shape
@@ -132,19 +133,108 @@
     for stage in stages:
         copies.append(list(enumerate(stage, sum(len(done) for done in copies))))
 
-    def each(items, sending, action):
-        for index, item in items:
-            if item[0] == "block":
-                action(copy_of(index, item))
+    flat = [pair for stage in copies for pair in stage]
+    odd = lax.rem(me, 2) == 1
+    even = lax.rem(me, 2) == 0
+
+    def direct_sender(item):
+        delta = item[1]
+        if delta % 2 == 0:
+            return (even, odd)
+        return (odd,) if delta == 1 else (even,) if delta == -1 else ()
+
+    def direct_receiver(item):
+        delta = item[1]
+        return (even,) if delta == 1 else (odd,) if delta == -1 else ()
+
+    def side_present(item, sending):
+        if item[0] == "block":
+            return None
+        return has_high if (item[0] == "down") == sending else has_low
+
+    def guarded(conditions, action):
+        conditions = [c for c in conditions if c is not None]
+        if not conditions:
+            action()
+        else:
+            pl.when(functools.reduce(jnp.logical_and, conditions))(action)
+
+    def window_part(item, slot_start):
+        kind, _, first, last = item
+        if kind == "block":
+            start = jnp.where(north, first, rows - last) + 1
+        else:
+            start = 0 if kind == "down" else rows + 1
+        return window.at[pl.ds(start, last - first), pl.ds(slot_start, cols)]
+
+    def receiver_side(item):
+        return has_low if item[0] == "down" else has_high if item[0] == "up" else None
+
+    def relay_of(index, item, target, held):
+        source = pl.multiple_of((middle + held) * cols, cols)
+        landing = ((item[1] + middle) % lon_count) * cols
+        return pltpu.make_async_remote_copy(
+            src_ref=window_part(item, source),
+            dst_ref=window_part(item, landing),
+            send_sem=relay_sem.at[index],
+            recv_sem=recv_sem.at[index],
+            device_id={"lon": target},
+            device_id_type=MESH,
+        )
+
+    def relay_action(index, item, action):
+        kind, delta, first, last = item
+        if delta % 2 == 0:
+            return
+        present = receiver_side(item)
+        if abs(delta) == 1 and kind == "block" and last <= counts[2] and last < rows:
+            parity = even if delta == 1 else odd
+            target = lax.rem(me + lon_count + delta, lon_count)
+            guarded([parity], lambda: action(relay_of(index, item, target, 2 * delta)))
+            return
+        for parity, own_delta in ((even, 1), (odd, -1)):
+            if delta == own_delta:
+                continue
+            target = lax.rem(me + 2 * lon_count - delta + own_delta, lon_count)
+            guarded(
+                [parity, present],
+                lambda: action(relay_of(index, item, target, own_delta)),
+            )
+
+    def send_direct(action):
+        for index, item in flat:
+            parities = direct_sender(item)
+            if len(parities) == 2:
+                guarded([side_present(item, True)], lambda: action(copy_of(index, item)))
             else:
-                present = has_high if (item[0] == "down") == sending else has_low
-
-                @pl.when(present)
-                def _():
-                    action(copy_of(index, item))
-
-    for stage in copies:
-        each(stage, True, lambda copy: copy.start())
+                for parity in parities:
+                    guarded(
+                        [parity, side_present(item, True)],
+                        lambda: action(copy_of(index, item)),
+                    )
+
+    def await_direct(stage):
+        for index, item in stage:
+            if item[1] in (2, -2) and item[0] == "block":
+                copy_of(index, item).wait_recv()
+            for parity in direct_receiver(item):
+                guarded(
+                    [parity, side_present(item, False)],
+                    lambda: copy_of(index, item).wait_recv(),
+                )
+
+    def await_rest(stage):
+        for index, item in stage:
+            side = side_present(item, False)
+            if item[1] in (2, -2) and item[0] == "block":
+                continue
+            if item[1] in (1, -1):
+                other = odd if item[1] == 1 else even
+                guarded([other, side], lambda: copy_of(index, item).wait_recv())
+            else:
+                guarded([side], lambda: copy_of(index, item).wait_recv())
+
+    send_direct(lambda copy: copy.start())
 
     window[1 : rows + 1, middle * cols : (middle + 1) * cols, :] = x_ref[...]
     for delta, count in counts.items():
@@ -204,6 +294,11 @@
 
     lax.fori_loop(0, bases, build, 0)
 
+    for stage in copies:
+        await_direct(stage)
+        for index, item in stage:
+            relay_action(index, item, lambda copy: copy.start())
+
     def group(low, high):
         start = jnp.where(north, low, rows - high)
         half = high - low
@@ -237,13 +332,14 @@
         out_ref[pl.ds(start, half)] = result.reshape(half, cols, channels)
 
     for stage, (low, high) in zip(copies, groups):
-        each(stage, False, lambda copy: copy.wait_recv())
+        await_rest(stage)
         if stage is copies[0]:
             for load in loads:
                 load.wait()
         group(low, high)
-    for stage in copies:
-        each(stage, True, lambda copy: copy.wait_send())
+    send_direct(lambda copy: copy.wait_send())
+    for index, item in flat:
+        relay_action(index, item, lambda copy: copy.wait_send())
 
 
 def on_device(
@@ -279,6 +375,7 @@
             pltpu.VMEM((hidden, channels), jnp.bfloat16),
             pltpu.SemaphoreType.DMA((count,)),
             pltpu.SemaphoreType.DMA((count,)),
+            pltpu.SemaphoreType.DMA((count,)),
             pltpu.SemaphoreType.DMA((3,)),
         ],
         compiler_params=pltpu.CompilerParams(

time: 34.5 us -> 37.1 us (1.075)
  the two profiles are of different devices: /device:TPU:0 before, /device:TPU:16 now
where the time goes in v3:
time: 37.1 us; the launch traced here: 36.9 us
  Pallas kernels  35.2 us (95%)
  local copies, waits for them, and re-layouts  1.73 us (5%)
    pallas_call x1, Pallas kernels, on_device(): pl.pallas_call(functools.partial(block_kernel, lon_count, lat_count, plan...  35.2 us
    unnamed x1, local copies, waits for them, and re-layouts  1.73 us

profile of v3, /device:TPU:16, one launch (start us, length us, event | category | flops | bytes accessed | tf_op | source)
XLA Modules:
  0.0 36.9 jit_solution(219724170679738965)
XLA Ops:
  0.0 35.2 %shard_map.82 = bf16[16,16,640]{2,1,0:T(8,128)(2,1)} custom-call(bf16[16,16,640]{2,1,0:T(8,128)(2,1)} %bitcast.8, s32[7,16,32]{2,1,0:T(8,128)} %bitcast.9, s32[7,16,32]{2,1,0:T(8,128)} %bitcast.10, f32[7,16,32]{2,1,0:T(8,128)} %bitcast.11, f32[640]{0:T(1024)} %gain_ref.1, bf16[4480,640]{1,0:T(8,128)(2,1)} %bitcast.6, bf16[640,1280]{1,0:T(8,128)(2,1)} %up_hbm.1, ...), custom_call_target="tpu_custom_call" | custom-call | tf_op jit(solution)/shard_map/pallas_call | solution.py:364
  35.2 1.7 %copy.10 = bf16[640,16,16]{0,2,1:T(8,128)(2,1)} copy(bf16[640,16,16]{0,2,1:T(8,128)(2,1)} %bitcast.7) | data formatting | bytes 655360

commit v4 on v2

--- a/solution.py
+++ b/solution.py
@@ -15,17 +15,27 @@
 def plan_copies(lon_count, lat_count, rows, cols):
     lon_total, row_total = lon_count * cols, lat_count * rows
 
+    def reach(row):
+        nearest = min(row + 1, row_total - row)
+        return min(lon_total // 2, 4 * row_total // nearest)
+
     def distance(row):
-        nearest = min(row + 1, row_total - row)
-        reach = min(lon_total // 2, 4 * row_total // nearest)
-        return min(-(-reach // cols), lon_count // 2)
+        return min(-(-reach(row) // cols), lon_count // 2)
+
+    def in_half(span, delta):
+        if delta == 0 or abs(delta) == lon_count // 2:
+            return False
+        return span - cols * (abs(delta) - 1) <= cols // 2
 
     need = [distance(max(p - 1, 0)) for p in range(rows)]
     deltas = [d for d in range(1 - lon_count // 2, lon_count // 2 + 1) if d != 0]
     counts = {delta: sum(1 for d in need if d >= abs(delta)) for delta in deltas}
-    edge = 0
+    spans = [reach(max(p - 1, 0)) for p in range(rows)]
+    fulls = {d: sum(1 for p in range(counts[d]) if not in_half(spans[p], d)) for d in deltas}
+    edge, edge_span = 0, 0
     for boundary in range(1, lat_count):
         edge = max(edge, distance(boundary * rows - 1), distance(boundary * rows))
+        edge_span = max(edge_span, reach(boundary * rows - 1), reach(boundary * rows))
     halo = [d for d in range(1 - lon_count // 2, lon_count // 2 + 1) if abs(d) <= edge]
     groups = [(rows // 2, rows), (rows // 4, rows // 2), (0, rows // 4)]
     stages = []
@@ -34,13 +44,19 @@
         lower = max(low - 1, 0)
         stage = []
         for delta in sorted(deltas, key=lambda d: -abs(d)):
-            if min(counts[delta], upper) > lower:
-                stage.append(("block", delta, lower, min(counts[delta], upper)))
+            full, top = min(fulls[delta], upper), min(counts[delta], upper)
+            if full > lower:
+                stage.append(("block", delta, lower, full, False))
+            if top > max(full, lower):
+                stage.append(("block", delta, max(full, lower), top, True))
         stages.append(stage)
         upper = lower
     if lat_count > 1:
-        stages[0] = [(side, d, 0, 1) for d in halo for side in ("down", "up")] + stages[0]
-    return groups, stages, counts, halo
+        stages[0] = [
+            (side, d, 0, 1, in_half(edge_span, d)) for d in halo for side in ("down", "up")
+        ] + stages[0]
+    halves = [d for d in halo if in_half(edge_span, d)]
+    return groups, stages, counts, fulls, halo, halves
 
 
 def block_kernel(
@@ -70,7 +86,7 @@
     bases, entries = rows_ref.shape[:2]
     lon_total = lon_count * cols
     middle = lon_count // 2
-    groups, stages, counts, halo = plan
+    groups, stages, counts, fulls, halo, halves = plan
     me, lat = lax.axis_index("lon"), lax.axis_index("lat")
     north = 2 * lat < lat_count
     has_low, has_high = lat > 0, lat < lat_count - 1
@@ -103,21 +119,24 @@
     pl.semaphore_wait(barrier, lon_count - 1 + sides * len(halo_deltas))
 
     def copy_of(index, item):
-        kind, delta, first, last = item
+        kind, delta, first, last, halved = item
+        width = cols // 2 if halved else cols
+        offset = cols // 2 if halved and delta < 0 else 0
         target = lax.rem(me + lon_count - delta, lon_count)
         slot = (delta + middle) % lon_count
+        here, there = pl.ds(offset, width), pl.ds(slot * cols + offset, width)
         if kind == "block":
             start = jnp.where(north, first, rows - last)
-            source = x_ref.at[pl.ds(start, last - first)]
-            landing = window.at[pl.ds(start + 1, last - first), pl.ds(slot * cols, cols)]
+            source = x_ref.at[pl.ds(start, last - first), here]
+            landing = window.at[pl.ds(start + 1, last - first), there]
             device = {"lon": target}
         elif kind == "down":
-            source = x_ref.at[pl.ds(rows - 1, 1)]
-            landing = window.at[pl.ds(0, 1), pl.ds(slot * cols, cols)]
+            source = x_ref.at[pl.ds(rows - 1, 1), here]
+            landing = window.at[pl.ds(0, 1), there]
             device = {"lon": target, "lat": jnp.minimum(lat + 1, lat_count - 1)}
         else:
-            source = x_ref.at[pl.ds(0, 1)]
-            landing = window.at[pl.ds(rows + 1, 1), pl.ds(slot * cols, cols)]
+            source = x_ref.at[pl.ds(0, 1), here]
+            landing = window.at[pl.ds(rows + 1, 1), there]
             device = {"lon": target, "lat": jnp.maximum(lat - 1, 0)}
         return pltpu.make_async_remote_copy(
             src_ref=source,
@@ -153,6 +172,17 @@
             gap = (rows - count, cols, channels)
             window[pl.ds(jnp.where(north, count, 0) + 1, rows - count),
                    slot * cols : (slot + 1) * cols] = jnp.zeros(gap, jnp.bfloat16)
+        partial = count - fulls[delta]
+        if partial > 0:
+            far = slot * cols + (0 if delta < 0 else cols // 2)
+            window[pl.ds(jnp.where(north, fulls[delta], rows - count) + 1, partial),
+                   far : far + cols // 2] = jnp.zeros(
+                (partial, cols // 2, channels), jnp.bfloat16
+            )
+    for delta in halves:
+        far = (delta + middle) % lon_count * cols + (0 if delta < 0 else cols // 2)
+        for line in (0, rows + 1):
+            window[line, far : far + cols // 2] = jnp.zeros((cols // 2, channels), jnp.bfloat16)
     for present, line in ((has_low, 0), (has_high, rows + 1)):
         for delta in range(1 - middle, middle + 1):
             slot = (delta + middle) % lon_count

time: 34.5 us -> 33.5 us (0.971)
  Pallas kernels: 32.6 us -> 31.6 us
    pallas_call x1, Pallas kernels: 32.6 us -> 31.6 us  [on_device(): pl.pallas_call(functools.partial(block_kernel, lon_count, lat_count, plan...]
where the time goes in v4:
time: 33.5 us; the launch traced here: 33.3 us
  Pallas kernels  31.6 us (94%)
  local copies, waits for them, and re-layouts  1.73 us (5%)
    pallas_call x1, Pallas kernels, on_device(): pl.pallas_call(functools.partial(block_kernel, lon_count, lat_count, plan...  31.6 us
    unnamed x1, local copies, waits for them, and re-layouts  1.73 us

profile of v4, /device:TPU:0, one launch (start us, length us, event | category | flops | bytes accessed | tf_op | source)
XLA Modules:
  0.0 33.3 jit_solution(7278787421888288701)
XLA Ops:
  0.0 31.6 %shard_map.82 = bf16[16,16,640]{2,1,0:T(8,128)(2,1)} custom-call(bf16[16,16,640]{2,1,0:T(8,128)(2,1)} %bitcast.8, s32[7,16,32]{2,1,0:T(8,128)} %bitcast.9, s32[7,16,32]{2,1,0:T(8,128)} %bitcast.10, f32[7,16,32]{2,1,0:T(8,128)} %bitcast.11, f32[640]{0:T(1024)} %gain_ref.1, bf16[4480,640]{1,0:T(8,128)(2,1)} %bitcast.6, bf16[640,1280]{1,0:T(8,128)(2,1)} %up_hbm.1, ...), custom_call_target="tpu_custom_call" | custom-call | tf_op jit(solution)/shard_map/pallas_call | solution.py:298
  31.6 1.7 %copy.10 = bf16[640,16,16]{0,2,1:T(8,128)(2,1)} copy(bf16[640,16,16]{0,2,1:T(8,128)(2,1)} %bitcast.7) | data formatting | bytes 655360

commit v5 on v4

--- a/solution.py
+++ b/solution.py
@@ -63,7 +63,7 @@
     lon_count,
     lat_count,
     plan,
-    x_ref,
+    x_hbm,
     rows_ref,
     lons_ref,
     weights_ref,
@@ -71,6 +71,8 @@
     mix_hbm,
     up_hbm,
     down_hbm,
+    out_hbm,
+    x_ref,
     out_ref,
     window,
     filters,
@@ -81,6 +83,7 @@
     send_sem,
     recv_sem,
     load_sem,
+    out_sem,
 ):
     rows, cols, channels = x_ref.shape
     bases, entries = rows_ref.shape[:2]
@@ -96,8 +99,8 @@
         pltpu.make_async_copy(up_hbm, up_ref, load_sem.at[1]),
         pltpu.make_async_copy(down_hbm, down_ref, load_sem.at[2]),
     ]
-    for load in loads:
-        load.start()
+    fetch = pltpu.make_async_copy(x_hbm, x_ref, load_sem.at[3])
+    fetch.start()
 
     barrier = pltpu.get_barrier_semaphore()
     halo_deltas = halo if lat_count > 1 else []
@@ -117,6 +120,7 @@
 
     sides = jnp.where(has_low, 1, 0) + jnp.where(has_high, 1, 0)
     pl.semaphore_wait(barrier, lon_count - 1 + sides * len(halo_deltas))
+    fetch.wait()
 
     def copy_of(index, item):
         kind, delta, first, last, halved = item
@@ -164,6 +168,8 @@
 
     for stage in copies:
         each(stage, True, lambda copy: copy.start())
+    for load in loads:
+        load.start()
 
     window[1 : rows + 1, middle * cols : (middle + 1) * cols, :] = x_ref[...]
     for delta, count in counts.items():
@@ -266,14 +272,21 @@
         result = (latent + lowered).astype(jnp.bfloat16)
         out_ref[pl.ds(start, half)] = result.reshape(half, cols, channels)
 
+    puts = []
     for stage, (low, high) in zip(copies, groups):
         each(stage, False, lambda copy: copy.wait_recv())
         if stage is copies[0]:
             for load in loads:
                 load.wait()
         group(low, high)
+        part = pl.ds(jnp.where(north, low, rows - high), high - low)
+        put = pltpu.make_async_copy(out_ref.at[part], out_hbm.at[part], out_sem.at[len(puts)])
+        put.start()
+        puts.append(put)
     for stage in copies:
         each(stage, True, lambda copy: copy.wait_send())
+    for put in puts:
+        put.wait()
 
 
 def on_device(
@@ -298,9 +311,11 @@
     result = pl.pallas_call(
         functools.partial(block_kernel, lon_count, lat_count, plan),
         out_shape=jax.ShapeDtypeStruct((rows, cols, channels), jnp.bfloat16),
-        in_specs=[in_vmem] * 5 + [anywhere] * 3,
-        out_specs=in_vmem,
+        in_specs=[anywhere] + [in_vmem] * 4 + [anywhere] * 3,
+        out_specs=anywhere,
         scratch_shapes=[
+            pltpu.VMEM((rows, cols, channels), jnp.bfloat16),
+            pltpu.VMEM((rows, cols, channels), jnp.bfloat16),
             pltpu.VMEM((rows + 2, lon_total, channels), jnp.bfloat16),
             pltpu.VMEM((rows, bases * cols, 3 * lon_total), jnp.bfloat16),
             pltpu.VMEM((rows // 2 * cols, bases * channels), jnp.bfloat16),
@@ -309,7 +324,8 @@
             pltpu.VMEM((hidden, channels), jnp.bfloat16),
             pltpu.SemaphoreType.DMA((count,)),
             pltpu.SemaphoreType.DMA((count,)),
-            pltpu.SemaphoreType.DMA((3,)),
+            pltpu.SemaphoreType.DMA((4,)),
+            pltpu.SemaphoreType.DMA((len(plan[0]),)),
         ],
         compiler_params=pltpu.CompilerParams(
             collective_id=0, has_side_effects=True, vmem_limit_bytes=56 * 1024 * 1024

time: 33.5 us -> 33.4 us (level)
  no operation moved by 1% of the time
where the time goes in v5:
time: 33.4 us; the launch traced here: 33.2 us
  Pallas kernels  31.4 us (94%)
  local copies, waits for them, and re-layouts  1.73 us (5%)
    pallas_call x1, Pallas kernels, on_device(): pl.pallas_call(functools.partial(block_kernel, lon_count, lat_count, plan...  31.4 us
    unnamed x1, local copies, waits for them, and re-layouts  1.73 us

profile of v5, /device:TPU:0, one launch (start us, length us, event | category | flops | bytes accessed | tf_op | source)
XLA Modules:
  0.0 33.2 jit_solution(18258631433436236371)
XLA Ops:
  0.0 31.4 %shard_map.82 = bf16[16,16,640]{2,1,0:T(8,128)(2,1)} custom-call(bf16[16,16,640]{2,1,0:T(8,128)(2,1)} %bitcast.8, s32[7,16,32]{2,1,0:T(8,128)} %bitcast.9, s32[7,16,32]{2,1,0:T(8,128)} %bitcast.10, f32[7,16,32]{2,1,0:T(8,128)} %bitcast.11, f32[640]{0:T(1024)} %gain_ref.1, bf16[4480,640]{1,0:T(8,128)(2,1)} %bitcast.6, bf16[640,1280]{1,0:T(8,128)(2,1)} %up_hbm.1, ...), custom_call_target="tpu_custom_call" | custom-call | tf_op jit(solution)/shard_map/pallas_call | solution.py:311
  31.4 1.7 %copy.10 = bf16[640,16,16]{0,2,1:T(8,128)(2,1)} copy(bf16[640,16,16]{0,2,1:T(8,128)(2,1)} %bitcast.7) | data formatting | bytes 655360
